TPU v7x, 32 devices: a whole 2x2x4 slice. The times are simulated.
32 devices in a mesh: section: 4 (over y, core), fsdp: 8 (over z, x).
Axes of the slice: x: 2, y: 2, z: 4, core: 2. Of those that a mesh axis runs over, the one named last changes fastest.
Arguments:
- hidden_in: bfloat16 [1024, 4096], P('fsdp'), may hold values from -6 to 6
- out_grad: bfloat16 [1024, 4096], P('fsdp'), may hold values from -6 to 6
- fast_in: float32 [4, 4096, 1024], P('section', 'fsdp'), may hold values from -6 to 6
- fast_out: float32 [4, 1024, 4096], P('section', None, 'fsdp'), may hold values from -6 to 6
- slow_in: float32 [4, 4096, 1024], P('section', 'fsdp'), may hold values from -6 to 6
- slow_out: float32 [4, 1024, 4096], P('section', None, 'fsdp'), may hold values from -6 to 6
Outputs:
- section_out: bfloat16 [4, 1024, 4096], P('section', 'fsdp')
- input_grad: bfloat16 [4, 1024, 4096], P('section', 'fsdp')
- synced_in: float32 [4, 4096, 1024], P('section', 'fsdp')
- synced_out: float32 [4, 1024, 4096], P('section', None, 'fsdp')
All inputs are finite; a program needn't handle non-finite values.
Results may differ from a plain program's by a relative error of at most 0.014.
Values may be sent and summed in bfloat16 or wider, within the bound.
No kernel may reach another device: no remote copies, remote signals or barrier semaphores. Data moves between devices by JAX's collectives and lax.ppermute only.
A program may use at most 896 MiB of HBM per device.

v0:
```python
import math
import jax
import jax.numpy as jnp
from jax import lax
from jax.sharding import PartitionSpec as P

epsilon = 1e-05
fast_rate = 0.5
preview_mix = 0.5


def from_behind(value, axis, steps):
    count = lax.axis_size(axis)
    leading, last = (max(0, -steps), min(count, count - steps))
    return lax.ppermute(value, axis, [(source, source + steps) for source in range(leading, last)])


def contract_last(left_rows, right_rows):
    return lax.dot_general(
        left_rows, right_rows, (((1,), (1,)), ((), ())), preferred_element_type=jnp.float32
    )


def contract_first(left_rows, right_rows):
    return lax.dot_general(
        left_rows, right_rows, (((0,), (0,)), ((), ())), preferred_element_type=jnp.float32
    )


def prepare(hidden, weight_in):
    widened = hidden.astype(jnp.float32)
    inverse_rms = lax.rsqrt(jnp.mean(widened * widened, axis=-1, keepdims=True) + epsilon)
    normed = (widened * inverse_rms).astype(jnp.bfloat16)
    pre_act = jnp.dot(normed, weight_in, preferred_element_type=jnp.float32)
    activated = jax.nn.silu(pre_act).astype(jnp.bfloat16)
    return (widened, inverse_rms, normed, pre_act, activated)


def advance(hidden, weight_in, weight_out):
    widened, inverse_rms, normed, pre_act, activated = prepare(hidden, weight_in)
    return (widened + jnp.dot(activated, weight_out, preferred_element_type=jnp.float32)).astype(
        jnp.bfloat16
    )


def retreat(hidden, cot_in, weight_in, weight_out):
    widened, inverse_rms, normed, pre_act, activated = prepare(hidden, weight_in)
    act_grad = contract_last(cot_in, weight_out)
    sigmoid_vals = jax.nn.sigmoid(pre_act)
    pre_grad = (act_grad * sigmoid_vals * (1.0 + pre_act * (1.0 - sigmoid_vals))).astype(
        jnp.bfloat16
    )
    norm_grad = contract_last(pre_grad, weight_in)
    unit_rows = widened * inverse_rms
    rms_grad = inverse_rms * (
        norm_grad - unit_rows * jnp.mean(norm_grad * unit_rows, axis=-1, keepdims=True)
    )
    earlier = (cot_in.astype(jnp.float32) + rms_grad).astype(jnp.bfloat16)
    return (earlier, contract_first(normed, pre_grad), contract_first(activated, cot_in))


def shards(hidden_in, out_grad, fast_in, fast_out, slow_in, slow_out):
    sections = lax.axis_size("section")
    section_index = lax.axis_index("section")
    row_count, model_width = hidden_in.shape
    branch_units = fast_in.shape[2]
    in_scale = 1.0 / math.sqrt(model_width)
    out_scale = 1.0 / math.sqrt(branch_units)
    local_in = (fast_in[0] * in_scale).astype(jnp.bfloat16)
    local_out = (fast_out[0] * out_scale).astype(jnp.bfloat16)
    weight_in, weight_out = (
        lax.all_gather(local_in, "fsdp", axis=0, tiled=True),
        lax.all_gather(local_out, "fsdp", axis=1, tiled=True),
    )
    portions = 1
    block_rows = row_count // portions
    turn_count = sections + portions - 1
    sources = hidden_in.reshape(portions, block_rows, model_width)
    targets = out_grad.reshape(portions, block_rows, model_width)
    saved_inputs = jnp.zeros_like(sources)
    produced = jnp.zeros_like(sources)
    incoming = jnp.zeros((block_rows, model_width), jnp.bfloat16)
    for timestep in range(turn_count):
        block_slot = timestep - section_index
        active = (block_slot >= 0) & (block_slot < portions)
        block_index = jnp.clip(block_slot, 0, portions - 1)
        first_input = lax.dynamic_index_in_dim(sources, block_index, 0, keepdims=False)
        section_input = jnp.where(section_index == 0, first_input, incoming)

        def run_forward():
            return advance(section_input, weight_in, weight_out)

        def skip_forward():
            return jnp.zeros_like(section_input)

        section_output = lax.cond(active, run_forward, skip_forward)
        saved_inputs = jnp.where(
            active,
            lax.dynamic_update_index_in_dim(saved_inputs, section_input, block_index, 0),
            saved_inputs,
        )
        produced = jnp.where(
            active,
            lax.dynamic_update_index_in_dim(produced, section_output, block_index, 0),
            produced,
        )
        if timestep + 1 < turn_count:
            incoming = from_behind(section_output, "section", 1)
    grad_in = jnp.zeros((model_width, branch_units), jnp.float32)
    grad_out = jnp.zeros((branch_units, model_width), jnp.float32)
    cotangents = jnp.zeros_like(sources)
    incoming = jnp.zeros((block_rows, model_width), jnp.bfloat16)
    for timestep in range(turn_count):
        block_slot = timestep - (sections - 1 - section_index)
        active = (block_slot >= 0) & (block_slot < portions)
        block_index = jnp.clip(block_slot, 0, portions - 1)
        last_cot = lax.dynamic_index_in_dim(targets, block_index, 0, keepdims=False)
        cot_in = jnp.where(section_index == sections - 1, last_cot, incoming)
        hidden = lax.dynamic_index_in_dim(saved_inputs, block_index, 0, keepdims=False)

        def run_backward():
            return retreat(hidden, cot_in, weight_in, weight_out)

        def skip_backward():
            return (
                jnp.zeros_like(cot_in),
                jnp.zeros((model_width, branch_units), jnp.float32),
                jnp.zeros((branch_units, model_width), jnp.float32),
            )

        earlier, term_in, term_out = lax.cond(active, run_backward, skip_backward)
        grad_in = grad_in + term_in
        grad_out = grad_out + term_out
        cotangents = jnp.where(
            active, lax.dynamic_update_index_in_dim(cotangents, earlier, block_index, 0), cotangents
        )
        if timestep + 1 < turn_count:
            incoming = from_behind(earlier, "section", -1)
    shard_in, shard_out = (
        lax.psum_scatter(
            (grad_in * in_scale).astype(jnp.bfloat16), "fsdp", scatter_dimension=0, tiled=True
        ).astype(jnp.float32),
        lax.psum_scatter(
            (grad_out * out_scale).astype(jnp.bfloat16), "fsdp", scatter_dimension=1, tiled=True
        ).astype(jnp.float32),
    )
    fresh_in = fast_in[0] - fast_rate * shard_in
    fresh_out = fast_out[0] - fast_rate * shard_out
    synced_first = slow_in[0] + preview_mix * (fresh_in - slow_in[0])
    synced_second = slow_out[0] + preview_mix * (fresh_out - slow_out[0])
    section_out = produced.reshape(row_count, model_width)[None]
    input_grad = cotangents.reshape(row_count, model_width)[None]
    return (section_out, input_grad, synced_first[None], synced_second[None])


def solution(mesh):
    placed = (
        P("fsdp", None),
        P("fsdp", None),
        P("section", "fsdp", None),
        P("section", None, "fsdp"),
        P("section", "fsdp", None),
        P("section", None, "fsdp"),
    )
    return jax.shard_map(
        shards,
        mesh=mesh,
        in_specs=placed,
        out_specs=(
            P("section", "fsdp", None),
            P("section", "fsdp", None),
            P("section", "fsdp", None),
            P("section", None, "fsdp"),
        ),
        check_vma=False,
    )
```

profile of v0, /device:TPU:0, one launch (start us, length us, event | category | flops | bytes accessed | tf_op | source)
XLA Modules:
  0.0 812.1 jit_solution(2471304480929756898)
XLA Ops:
  7.2 3.0 fusion.125
  10.2 0.0 all-gather.5.cloned.1.call-start
  10.3 1.2 fusion.124
  11.5 0.0 reduce-scatter.5.cloned.1.call-start
  11.6 0.1 broadcast_select_fusion.7
  11.7 126.2 %all-gather.3.cloned.1.call-done = bf16[4096,1024]{1,0:T(8,128)(2,1)} async-done(((bf16[512,1024]{1,0:T(8,128)(2,1)}), bf16[4096,1024]{1,0:T(8,128)(2,1)}) %all-gather.3.cloned.1.call-update) | async-done | bytes 8388624 | tf_op jit(solution)/shard_map/all_gather | solution.py:72
  137.9 125.8 %all-gather.5.cloned.1.call-done = bf16[1024,4096]{1,0:T(8,128)(2,1)} async-done(((bf16[1024,512]{1,0:T(8,128)(2,1)}), bf16[1024,4096]{1,0:T(8,128)(2,1)}) %all-gather.5.cloned.1.call-update) | async-done | bytes 8388624 | tf_op jit(solution)/shard_map/all_gather | solution.py:73
  263.7 8.6 %conditional.8 = (bf16[128,4096]{1,0:T(8,128)(2,1)S(1)}) conditional(s32[]{:T(128)} %convert_element_type.165, () %tuple.67, (bf16[128,4096]{1,0:T(8,128)(2,1)S(1)}, bf16[4096,1024]{1,0:T(8,128)(2,1)}, bf16[1024,4096]{1,0:T(8,128)(2,1)}) %tuple.68), branch_computations={%region_0.1_spmd, %region_1.3_spmd} | conditional | flops 2152857600 | bytes 19925000 | solution.py:96
  263.7 0.3 fusion.1
  264.0 8.3 %fusion = bf16[128,4096]{1,0:T(8,128)(2,1)S(1)} fusion(bf16[1024,4096]{1,0:T(8,128)(2,1)} %get-tuple-element.94, bf16[128,4096]{1,0:T(8,128)(2,1)S(1)} %get-tuple-element.92, bf16[4096,1024]{1,0:T(8,128)(2,1)} %get-tuple-element.93, f32[128]{0:T(128)S(1)} %add_rsqrt_fusion), kind=kOutput, calls=%fused_computation.1 | convolution fusion | flops 2151284736 | bytes 18874880 | tf_op jit(solution)/shard_map/cond/branch_1_fun/dot_general | solution.py:41
  272.3 1.4 collective-permute-start
  273.7 2.2 collective-permute-done
  275.8 1.1 broadcast_select_fusion.6
  276.9 0.1 conditional.9
  276.9 0.1 broadcast.218
  277.1 15.4 %collective-permute-start.1 = (bf16[128,4096]{1,0:T(8,128)(2,1)S(1)}, bf16[128,4096]{1,0:T(8,128)(2,1)S(1)}, u32[]{:S(2)}, u32[]{:S(2)}) collective-permute-start(bf16[128,4096]{1,0:T(8,128)(2,1)S(1)} %get-tuple-element.193), channel_id=1, source_target_pairs={{0,8},{8,16},{16,24},{1,9},{9,17},{17,25},{2,10},{10,18},{18,26},{... | collective-permute-start | bytes 3145736 | tf_op jit(solution)/shard_map/ppermute | solution.py:15
  292.5 2.2 collective-permute-done.1
  294.7 1.1 broadcast_select_fusion.5
  295.8 0.1 conditional.10
  295.8 0.1 broadcast.221
  295.9 12.4 %collective-permute-start.2 = (bf16[128,4096]{1,0:T(8,128)(2,1)S(1)}, bf16[128,4096]{1,0:T(8,128)(2,1)}, u32[]{:S(2)}, u32[]{:S(2)}) collective-permute-start(bf16[128,4096]{1,0:T(8,128)(2,1)S(1)} %get-tuple-element.194), channel_id=1, source_target_pairs={{0,8},{8,16},{16,24},{1,9},{9,17},{17,25},{2,10},{10,18},{18,26},{... | collective-permute-start | bytes 3145736 | tf_op jit(solution)/shard_map/ppermute | solution.py:15
  308.3 1.4 collective-permute-done.2
  309.7 1.2 select_select_fusion
  310.9 0.1 broadcast.254
  311.0 16.0 %conditional.12 = (bf16[128,4096]{1,0:T(8,128)(2,1)S(1)}, f32[4096,1024]{1,0:T(8,128)}, f32[1024,4096]{1,0:T(8,128)}) conditional(s32[]{:T(128)} %convert_element_type.171, () %tuple.75, (pred[]{:T(512)}, bf16[128,4096]{1,0:T(8,128)(2,1)S(1)}, bf16[128,4096]{1,0:T(8,128)(2,1)S(1)}, bf16[128,4096]{1,0:T(8,128)(2,1)S(1)}, ...), branch_computations={%region_12.13_spmd, %region_13.16_spmd} | conditional | flops 5382078464 | bytes 136582752 | solution.py:131
  311.0 0.1 broadcast.227
  311.1 7.8 broadcast.229
  318.9 7.9 broadcast.228
  327.0 1.3 collective-permute-start.3
  328.3 26.4 %collective-permute-done.3 = bf16[128,4096]{1,0:T(8,128)(2,1)} collective-permute-done((bf16[128,4096]{1,0:T(8,128)(2,1)S(1)}, bf16[128,4096]{1,0:T(8,128)(2,1)}, u32[]{:S(2)}, u32[]{:S(2)}) %collective-permute-start.3) | collective-permute-done | bytes 1048608 | tf_op jit(solution)/shard_map/ppermute | solution.py:15
  354.7 17.1 %conditional.13 = (bf16[128,4096]{1,0:T(8,128)(2,1)}, f32[4096,1024]{1,0:T(8,128)}, f32[1024,4096]{1,0:T(8,128)}) conditional(s32[]{:T(128)} %convert_element_type.170, () %tuple.74, (pred[]{:T(512)}, bf16[128,4096]{1,0:T(8,128)(2,1)S(1)}, bf16[128,4096]{1,0:T(8,128)(2,1)}, bf16[128,4096]{1,0:T(8,128)(2,1)S(1)}, bf16[1024,4096]{1,0:T(8,128)(2,1)}, ...), branch_computations={%region_16.17_spmd, %region_17.20_spmd} | conditional | flops 5382078464 | bytes 136582752 | solution.py:131
  354.7 1.1 broadcast.233
  355.8 7.8 broadcast.235
  363.6 7.9 broadcast.234
  371.9 1.3 collective-permute-start.4
  373.2 15.8 %collective-permute-done.4 = bf16[128,4096]{1,0:T(8,128)(2,1)S(1)} collective-permute-done((bf16[128,4096]{1,0:T(8,128)(2,1)}, bf16[128,4096]{1,0:T(8,128)(2,1)S(1)}, u32[]{:S(2)}, u32[]{:S(2)}) %collective-permute-start.4) | collective-permute-done | bytes 1048608 | tf_op jit(solution)/shard_map/ppermute | solution.py:15
  389.0 16.1 %conditional.14 = (bf16[128,4096]{1,0:T(8,128)(2,1)S(1)}, f32[4096,1024]{1,0:T(8,128)}, f32[1024,4096]{1,0:T(8,128)}) conditional(s32[]{:T(128)} %convert_element_type.169, () %tuple.73, (pred[]{:T(512)}, bf16[128,4096]{1,0:T(8,128)(2,1)S(1)}, bf16[128,4096]{1,0:T(8,128)(2,1)S(1)}, bf16[128,4096]{1,0:T(8,128)(2,1)S(1)}, ...), branch_computations={%region_20.21_spmd, %region_21.24_spmd} | conditional | flops 5382078464 | bytes 136582752 | solution.py:131
  389.2 0.1 broadcast.239
  389.3 7.9 broadcast.241
  397.2 7.9 broadcast.240
  405.2 1.3 collective-permute-start.5
  406.5 41.1 %collective-permute-done.5 = bf16[128,4096]{1,0:T(8,128)(2,1)} collective-permute-done((bf16[128,4096]{1,0:T(8,128)(2,1)S(1)}, bf16[128,4096]{1,0:T(8,128)(2,1)}, u32[]{:S(2)}, u32[]{:S(2)}) %collective-permute-start.5) | collective-permute-done | bytes 1048608 | tf_op jit(solution)/shard_map/ppermute | solution.py:15
  447.6 31.9 %conditional.15 = (bf16[128,4096]{1,0:T(8,128)(2,1)}, f32[4096,1024]{1,0:T(8,128)}, f32[1024,4096]{1,0:T(8,128)}) conditional(s32[]{:T(128)} %convert_element_type.168, () %tuple.72, (pred[]{:T(512)}, bf16[128,4096]{1,0:T(8,128)(2,1)S(1)}, bf16[128,4096]{1,0:T(8,128)(2,1)}, bf16[128,4096]{1,0:T(8,128)(2,1)S(1)}, bf16[1024,4096]{1,0:T(8,128)(2,1)}, ...), branch_computations={%region_24.25_spmd, %region_25.28_spmd} | conditional | flops 5382078464 | bytes 136582752 | solution.py:131
  447.8 1.3 broadcast_select_fusion.3
  449.1 0.3 fusion.110
  449.4 4.8 fusion.115
  454.3 1.1 copy-done.15
  455.4 2.9 fusion.112
  458.3 3.0 fusion.105
  461.3 1.6 fusion.109
  462.9 8.1 fusion.117
  471.0 8.2 %fusion.113 = f32[4096,1024]{1,0:T(8,128)} fusion(bf16[128,1024]{1,0:T(8,128)(2,1)S(1)} %fusion.112, bf16[128,4096]{1,0:T(8,128)(2,1)S(1)} %get-tuple-element.125, f32[128]{0:T(128)S(1)} %add_rsqrt_fusion.7), kind=kOutput, calls=%fused_computation.137 | convolution fusion | flops 1075314688 | bytes 18088448 | tf_op jit(solution)/shard_map/cond/branch_1_fun/dot_general | solution.py:25
  479.4 25.8 %multiply_convert_fusion.12 = bf16[1024,4096]{1,0:T(8,128)(2,1)} fusion(f32[1024,4096]{1,0:T(8,128)} %get-tuple-element.155, f32[1024,4096]{1,0:T(8,128)} %get-tuple-element.154, f32[1024,4096]{1,0:T(8,128)} %get-tuple-element.152, f32[1024,4096]{1,0:T(8,128)} %get-tuple-element.153), kind=kLoop, calls=%fused_computation.144 | loop fusion | flops 20971520 | bytes 75497472 | tf_op jit(solution)/shard_map/convert_element_type | solution.py:144
  505.3 26.9 %multiply_convert_fusion.13 = bf16[4096,1024]{1,0:T(8,128)(2,1)} fusion(f32[4096,1024]{1,0:T(8,128)} %get-tuple-element.151, f32[4096,1024]{1,0:T(8,128)} %get-tuple-element.150, f32[4096,1024]{1,0:T(8,128)} %get-tuple-element.148, f32[4096,1024]{1,0:T(8,128)} %get-tuple-element.149), kind=kLoop, calls=%fused_computation.145 | loop fusion | flops 20971520 | bytes 75497472 | tf_op jit(solution)/shard_map/convert_element_type | solution.py:141
  532.2 1.2 copy-done.11
  533.4 0.1 conditional.11
  533.4 0.1 broadcast.224
  533.5 1.0 copy-done.10
  534.4 0.6 copy-done.5
  535.0 3.4 select_bitcast_fusion
  538.4 112.1 %reduce-scatter.5.cloned.1.call-done = bf16[1024,512]{1,0:T(8,128)(2,1)} async-done(((bf16[1024,4096]{1,0:T(8,128)(2,1)}), bf16[1024,512]{1,0:T(8,128)(2,1)}) %reduce-scatter.5.cloned.1.call-update) | async-done | bytes 1048592 | tf_op jit(solution)/shard_map/reduce_scatter | solution.py:143
  650.5 3.8 fusion.121
  654.2 146.3 %reduce-scatter.3.cloned.1.call-done = bf16[512,1024]{1,0:T(8,128)(2,1)} async-done(((bf16[4096,1024]{1,0:T(8,128)(2,1)}), bf16[512,1024]{1,0:T(8,128)(2,1)}) %reduce-scatter.3.cloned.1.call-update) | async-done | bytes 1048592 | tf_op jit(solution)/shard_map/reduce_scatter | solution.py:140
  800.6 4.6 fusion.123
  (36 shorter events, 0.2 us)
Async XLA Ops:
  7.2 3.1 copy-start.2
  7.2 130.7 %all-gather.3.cloned.1.call-start = ((), (), s32[]{:S(2)}) async-start(), calls=%async_computation.2 | async-start | bytes 9437184 | tf_op jit(solution)/shard_map/all_gather | solution.py:72
  10.2 1.4 copy-start.1
  10.2 253.5 %all-gather.5.cloned.1.call-start = ((), (), s32[]{:S(2)}) async-start(), calls=%async_computation.3 | async-start | bytes 9437184 | tf_op jit(solution)/shard_map/all_gather | solution.py:73
  11.5 638.9 %reduce-scatter.5.cloned.1.call-start = ((), (), s32[]{:S(2)}) async-start(), calls=%async_computation.5 | async-start | bytes 9437184 | tf_op jit(solution)/shard_map/reduce_scatter | solution.py:143
  272.3 4.7 copy-start.7
  272.3 3.6 collective-permute-start
  277.0 18.7 %copy-start.8 = (bf16[128,4096]{1,0:T(8,128)(2,1)}, bf16[128,4096]{1,0:T(8,128)(2,1)S(1)}, u32[]{:S(2)}) copy-start(bf16[128,4096]{1,0:T(8,128)(2,1)S(1)} %get-tuple-element.193) | copy-start | bytes 3145732
  277.1 17.6 %collective-permute-start.1 = (bf16[128,4096]{1,0:T(8,128)(2,1)S(1)}, bf16[128,4096]{1,0:T(8,128)(2,1)S(1)}, u32[]{:S(2)}, u32[]{:S(2)}) collective-permute-start(bf16[128,4096]{1,0:T(8,128)(2,1)S(1)} %get-tuple-element.193), channel_id=1, source_target_pairs={{0,8},{8,16},{16,24},{1,9},{9,17},{17,25},{2,10},{10,18},{18,26},{... | collective-permute-start | bytes 3145736 | tf_op jit(solution)/shard_map/ppermute | solution.py:15
  295.9 12.4 %copy-start.9 = (bf16[128,4096]{1,0:T(8,128)(2,1)}, bf16[128,4096]{1,0:T(8,128)(2,1)S(1)}, u32[]{:S(2)}) copy-start(bf16[128,4096]{1,0:T(8,128)(2,1)S(1)} %get-tuple-element.194) | copy-start | bytes 3145732
  295.9 13.8 %collective-permute-start.2 = (bf16[128,4096]{1,0:T(8,128)(2,1)S(1)}, bf16[128,4096]{1,0:T(8,128)(2,1)}, u32[]{:S(2)}, u32[]{:S(2)}) collective-permute-start(bf16[128,4096]{1,0:T(8,128)(2,1)S(1)} %get-tuple-element.194), channel_id=1, source_target_pairs={{0,8},{8,16},{16,24},{1,9},{9,17},{17,25},{2,10},{10,18},{18,26},{... | collective-permute-start | bytes 3145736 | tf_op jit(solution)/shard_map/ppermute | solution.py:15
  308.3 2.7 copy-start
  327.0 27.8 %copy-start.4 = (bf16[128,4096]{1,0:T(8,128)(2,1)}, bf16[128,4096]{1,0:T(8,128)(2,1)S(1)}, u32[]{:S(2)}) copy-start(bf16[128,4096]{1,0:T(8,128)(2,1)S(1)} %get-tuple-element.144) | copy-start | bytes 3145732
  327.0 27.8 %collective-permute-start.3 = (bf16[128,4096]{1,0:T(8,128)(2,1)S(1)}, bf16[128,4096]{1,0:T(8,128)(2,1)}, u32[]{:S(2)}, u32[]{:S(2)}) collective-permute-start(bf16[128,4096]{1,0:T(8,128)(2,1)S(1)} %get-tuple-element.144), channel_id=1, source_target_pairs={{8,0},{16,8},{24,16},{9,1},{17,9},{25,17},{10,2},{18,10},{26,18},{... | collective-permute-start | bytes 3145736 | tf_op jit(solution)/shard_map/ppermute | solution.py:15
  371.9 17.2 %collective-permute-start.4 = (bf16[128,4096]{1,0:T(8,128)(2,1)}, bf16[128,4096]{1,0:T(8,128)(2,1)S(1)}, u32[]{:S(2)}, u32[]{:S(2)}) collective-permute-start(bf16[128,4096]{1,0:T(8,128)(2,1)} %get-tuple-element.145), channel_id=1, source_target_pairs={{8,0},{16,8},{24,16},{9,1},{17,9},{25,17},{10,2},{18,10},{26,18},{... | collective-permute-start | bytes 3145736 | tf_op jit(solution)/shard_map/ppermute | solution.py:15
  405.2 42.4 %copy-start.6 = (bf16[128,4096]{1,0:T(8,128)(2,1)}, bf16[128,4096]{1,0:T(8,128)(2,1)S(1)}, u32[]{:S(2)}) copy-start(bf16[128,4096]{1,0:T(8,128)(2,1)S(1)} %get-tuple-element.146) | copy-start | bytes 3145732
  405.2 42.4 %collective-permute-start.5 = (bf16[128,4096]{1,0:T(8,128)(2,1)S(1)}, bf16[128,4096]{1,0:T(8,128)(2,1)}, u32[]{:S(2)}, u32[]{:S(2)}) collective-permute-start(bf16[128,4096]{1,0:T(8,128)(2,1)S(1)} %get-tuple-element.146), channel_id=1, source_target_pairs={{8,0},{16,8},{24,16},{9,1},{17,9},{25,17},{10,2},{18,10},{26,18},{... | collective-permute-start | bytes 3145736 | tf_op jit(solution)/shard_map/ppermute | solution.py:15
  449.1 9.2 %slice-start.6 = ((s8[8388608]{0:T(1024)(128)(4,1)}), s8[4194304]{0:T(1024)(128)(4,1)S(1)}, s32[]{:S(2)}) async-start(s8[8388608]{0:T(1024)(128)(4,1)} %bitcast.82), calls=%async_computation.12 | async-start | bytes 8388608 | tf_op jit(solution)/shard_map/cond
  449.4 5.9 copy-start.15
  449.4 8.9 %slice-start.7 = ((s8[8388608]{0:T(1024)(128)(4,1)}), s8[4194304]{0:T(1024)(128)(4,1)S(1)}, s32[]{:S(2)}) async-start(s8[8388608]{0:T(1024)(128)(4,1)} %bitcast.82), calls=%async_computation.13 | async-start | bytes 8388608 | tf_op jit(solution)/shard_map/cond
  505.2 295.3 %reduce-scatter.3.cloned.1.call-start = ((), (), s32[]{:S(2)}) async-start(), calls=%async_computation.4 | async-start | bytes 9437184 | tf_op jit(solution)/shard_map/reduce_scatter | solution.py:140
  532.1 1.2 copy-start.11
  533.4 1.6 copy-start.5
  533.5 1.0 copy-start.10
  535.0 115.5 %copy-start.3 = (f32[1,1024,512]{2,1,0:T(8,128)S(1)}, f32[1,1024,512]{2,1,0:T(8,128)}, u32[]{:S(2)}) copy-start(f32[1,1024,512]{2,1,0:T(8,128)} %param.25) | copy-start | bytes 6291460
Sparse Core Ops, SparseCore 0:
  10.7 127.1 all-gather.2
  140.5 123.1 all-gather.4
  505.4 145.0 reduce-scatter.4
  654.0 146.5 reduce-scatter.2
where the time goes:
time: 821 us; the launch traced here: 812 us
  waiting for transfers between devices  600 us (73%)
  other arithmetic  75.5 us (9%)
  local copies, waits for them, and re-layouts  52.8 us (6%)
  matrix products  35.3 us (4%)
  starting transfers between devices  33.2 us (4%)
  between operations  14.5 us (2%)
    reduce_scatter x1, waiting for transfers between devices, shards(): lax.psum_scatter((grad_in * in_scale).astype(jnp.bfloat16), 'fsdp', scatt...  146 us
    all_gather x1, waiting for transfers between devices, shards(): lax.all_gather(local_in, 'fsdp', axis=0, tiled=True)  126 us
    all_gather x1, waiting for transfers between devices, shards(): lax.all_gather(local_out, 'fsdp', axis=1, tiled=True)  126 us
    reduce_scatter x1, waiting for transfers between devices, shards(): lax.psum_scatter((grad_out * out_scale).astype(jnp.bfloat16), 'fsdp', sca...  112 us
    ppermute x6, waiting for transfers between devices, from_behind(): lax.ppermute(value, axis, [(source, source + steps) for source in range(l...  89.1 us
    another operation x13, local copies, waits for them, and re-layouts  48.9 us
    ppermute x6, starting transfers between devices, from_behind(): lax.ppermute(value, axis, [(source, source + steps) for source in range(l...  33 us
    convert_element_type x1, other arithmetic, shards(): (grad_in * in_scale).astype(jnp.bfloat16)  26.9 us
  transfers between devices with their start and end apart: 10, of which 10 were waited for; matrix products, arithmetic and copies ran while one was open for 4% of the time, Pallas kernels for 0%

commit v1 on v0

--- a/solution.py
+++ b/solution.py
@@ -7,6 +7,28 @@
 epsilon = 1e-05
 fast_rate = 0.5
 preview_mix = 0.5
+
+
+def laid_out(blocks, dim):
+    blocks = jnp.moveaxis(blocks, 0, dim)
+    shape = blocks.shape
+    return blocks.reshape(*shape[:dim], shape[dim] * shape[dim + 1], *shape[dim + 2 :])
+
+
+def grow_blocks(value, axis):
+    size = lax.axis_size(axis)
+    blocks = value[None]
+    for level in range(size.bit_length() - 1):
+        bit = 1 << level
+        other = lax.ppermute(blocks, axis, [(i, i ^ bit) for i in range(size)])
+        both = jnp.stack([blocks, other])
+        upper = lax.axis_index(axis) >> level & 1
+        blocks = jnp.where(upper == 0, both, both[::-1]).reshape(-1, *value.shape)
+    return blocks
+
+
+def collect(shard, axis, dim):
+    return laid_out(grow_blocks(shard, axis), dim)
 
 
 def from_behind(value, axis, steps):
@@ -69,7 +91,7 @@
     local_in = (fast_in[0] * in_scale).astype(jnp.bfloat16)
     local_out = (fast_out[0] * out_scale).astype(jnp.bfloat16)
     weight_in, weight_out = (
-        lax.all_gather(local_in, "fsdp", axis=0, tiled=True),
+        collect(local_in, "fsdp", 0),
         lax.all_gather(local_out, "fsdp", axis=1, tiled=True),
     )
     portions = 1

time: 821 us -> 943 us (1.15)
  waiting for transfers between devices: 600 us -> 689 us
  other arithmetic: 75.5 us -> 104 us
    ppermute x0 -> x3, waiting for transfers between devices: none -> 341 us  [grow_blocks(): other = lax.ppermute(blocks, axis, [(i, i ^ bit) for i in range(size)])]
    all_gather x1 -> x0, waiting for transfers between devices: 126 us -> none  [shards(): lax.all_gather(local_in, 'fsdp', axis=0, tiled=True)]
    all_gather x1, waiting for transfers between devices: 126 us -> 0.01 us  [shards(): lax.all_gather(local_out, 'fsdp', axis=1, tiled=True)]
    select_n x0 -> x2, other arithmetic: none -> 16.9 us  [grow_blocks(): blocks = jnp.where(upper == 0, both, both[::-1]).reshape(-1, *value.shape)]
    another operation x0 -> x4, other arithmetic: none -> 13.1 us  [grow_blocks(): both = jnp.stack([blocks, other])]
  transfers between devices with their start and end apart: 10 -> 12, of which waited for: 10 -> 11; matrix products, arithmetic and copies ran while one was open for 4% -> 7% of each run, Pallas kernels for 0% -> 0%
where the time goes in v1:
time: 943 us; the launch traced here: 934 us
  waiting for transfers between devices  689 us (73%)
  other arithmetic  104 us (11%)
  local copies, waits for them, and re-layouts  51.9 us (6%)
  starting transfers between devices  38.3 us (4%)
  matrix products  35.3 us (4%)
  between operations  14.5 us (2%)
    ppermute x3, waiting for transfers between devices, grow_blocks(): other = lax.ppermute(blocks, axis, [(i, i ^ bit) for i in range(size)])  341 us
    reduce_scatter x1, waiting for transfers between devices, shards(): lax.psum_scatter((grad_in * in_scale).astype(jnp.bfloat16), 'fsdp', scatt...  146 us
    reduce_scatter x1, waiting for transfers between devices, shards(): lax.psum_scatter((grad_out * out_scale).astype(jnp.bfloat16), 'fsdp', sca...  112 us
    ppermute x6, waiting for transfers between devices, from_behind(): lax.ppermute(value, axis, [(source, source + steps) for source in range(l...  89.1 us
    another operation x13, local copies, waits for them, and re-layouts  49.9 us
    ppermute x6, starting transfers between devices, from_behind(): lax.ppermute(value, axis, [(source, source + steps) for source in range(l...  33.2 us
    convert_element_type x1, other arithmetic, shards(): (grad_in * in_scale).astype(jnp.bfloat16)  27 us
    convert_element_type x1, other arithmetic, shards(): (grad_out * out_scale).astype(jnp.bfloat16)  25.8 us
  transfers between devices with their start and end apart: 12, of which 11 were waited for; matrix products, arithmetic and copies ran while one was open for 7% of the time, Pallas kernels for 0%

profile of v1, /device:TPU:0, one launch (start us, length us, event | category | flops | bytes accessed | tf_op | source)
XLA Modules:
  0.0 934.4 jit_solution(16133485487923479517)
XLA Ops:
  7.2 3.0 fusion.126
  10.3 0.2 multiply_convert_fusion.14
  10.5 3.0 collective-permute-start
  13.6 0.3 fusion.165
  13.8 34.2 %collective-permute-done = bf16[1,512,1024]{2,1,0:T(8,128)(2,1)} collective-permute-done((bf16[1,512,1024]{2,1,0:T(8,128)(2,1)S(1)}, bf16[1,512,1024]{2,1,0:T(8,128)(2,1)}, u32[]{:S(2)}, u32[]{:S(2)}) %collective-permute-start) | collective-permute-done | bytes 1048608 | tf_op jit(solution)/shard_map/ppermute | solution.py:23
  48.1 1.4 pad_maximum_fusion.2
  49.5 2.2 fusion.128
  51.7 1.8 collective-permute-start.1
  53.5 95.5 %collective-permute-done.1 = bf16[2,512,1024]{2,1,0:T(8,128)(2,1)} collective-permute-done((bf16[2,512,1024]{2,1,0:T(8,128)(2,1)}, bf16[2,512,1024]{2,1,0:T(8,128)(2,1)}, u32[]{:S(2)}, u32[]{:S(2)}) %collective-permute-start.1) | collective-permute-done | bytes 2097184 | tf_op jit(solution)/shard_map/ppermute | solution.py:23
  149.0 2.0 pad_maximum_fusion.1
  151.0 3.2 reverse_select_fusion.1
  154.2 0.2 collective-permute-start.2
  154.5 211.7 %collective-permute-done.2 = bf16[4,512,1024]{2,1,0:T(8,128)(2,1)} collective-permute-done((bf16[4,512,1024]{2,1,0:T(8,128)(2,1)}, bf16[4,512,1024]{2,1,0:T(8,128)(2,1)}, u32[]{:S(2)}, u32[]{:S(2)}) %collective-permute-start.2) | collective-permute-done | bytes 4194336 | tf_op jit(solution)/shard_map/ppermute | solution.py:23
  366.2 7.5 pad_maximum_fusion
  373.7 13.7 %reverse_select_fusion = bf16[2,4,512,1024]{3,2,1,0:T(8,128)(2,1)} fusion(bf16[2,4,512,1024]{3,2,1,0:T(8,128)(2,1)} %pad_maximum_fusion, pred[]{:T(512)S(6)} %eq.22), kind=kLoop, calls=%fused_computation.146 | loop fusion | flops 4194304 | bytes 16777216 | tf_op jit(solution)/shard_map/jit(_where)/select_n | solution.py:26
  387.3 8.6 conditional.8
  387.3 0.3 fusion.1
  387.6 8.3 fusion
  395.9 1.5 collective-permute-start.3
  397.5 2.2 collective-permute-done.3
  399.7 1.1 broadcast_select_fusion.6
  400.9 15.4 %collective-permute-start.4 = (bf16[128,4096]{1,0:T(8,128)(2,1)S(1)}, bf16[128,4096]{1,0:T(8,128)(2,1)S(1)}, u32[]{:S(2)}, u32[]{:S(2)}) collective-permute-start(bf16[128,4096]{1,0:T(8,128)(2,1)S(1)} %get-tuple-element.195), channel_id=1, source_target_pairs={{0,8},{8,16},{16,24},{1,9},{9,17},{17,25},{2,10},{10,18},{18,26},{... | collective-permute-start | bytes 3145736 | tf_op jit(solution)/shard_map/ppermute | solution.py:37
  416.3 2.2 collective-permute-done.4
  418.5 1.1 broadcast_select_fusion.5
  419.7 12.4 %collective-permute-start.5 = (bf16[128,4096]{1,0:T(8,128)(2,1)S(1)}, bf16[128,4096]{1,0:T(8,128)(2,1)}, u32[]{:S(2)}, u32[]{:S(2)}) collective-permute-start(bf16[128,4096]{1,0:T(8,128)(2,1)S(1)} %get-tuple-element.196), channel_id=1, source_target_pairs={{0,8},{8,16},{16,24},{1,9},{9,17},{17,25},{2,10},{10,18},{18,26},{... | collective-permute-start | bytes 3145736 | tf_op jit(solution)/shard_map/ppermute | solution.py:37
  432.1 1.4 collective-permute-done.5
  433.5 1.2 select_select_fusion
  434.8 16.0 %conditional.12 = (bf16[128,4096]{1,0:T(8,128)(2,1)S(1)}, f32[4096,1024]{1,0:T(8,128)}, f32[1024,4096]{1,0:T(8,128)}) conditional(s32[]{:T(128)} %convert_element_type.183, () %tuple.75, (pred[]{:T(512)}, bf16[128,4096]{1,0:T(8,128)(2,1)S(1)}, bf16[128,4096]{1,0:T(8,128)(2,1)S(1)}, bf16[128,4096]{1,0:T(8,128)(2,1)S(1)}, ...), branch_computations={%region_12.13_spmd, %region_13.16_spmd} | conditional | flops 5382078464 | bytes 136582752 | solution.py:153
  434.9 7.8 broadcast.239
  442.7 7.9 broadcast.238
  450.8 1.3 collective-permute-start.6
  452.1 26.4 %collective-permute-done.6 = bf16[128,4096]{1,0:T(8,128)(2,1)} collective-permute-done((bf16[128,4096]{1,0:T(8,128)(2,1)S(1)}, bf16[128,4096]{1,0:T(8,128)(2,1)}, u32[]{:S(2)}, u32[]{:S(2)}) %collective-permute-start.6) | collective-permute-done | bytes 1048608 | tf_op jit(solution)/shard_map/ppermute | solution.py:37
  478.6 17.2 %conditional.13 = (bf16[128,4096]{1,0:T(8,128)(2,1)}, f32[4096,1024]{1,0:T(8,128)}, f32[1024,4096]{1,0:T(8,128)}) conditional(s32[]{:T(128)} %convert_element_type.182, () %tuple.74, (pred[]{:T(512)}, bf16[128,4096]{1,0:T(8,128)(2,1)S(1)}, bf16[128,4096]{1,0:T(8,128)(2,1)}, bf16[128,4096]{1,0:T(8,128)(2,1)S(1)}, bf16[1024,4096]{1,0:T(8,128)(2,1)}, ...), branch_computations={%region_16.17_spmd, %region_17.20_spmd} | conditional | flops 5382078464 | bytes 136582752 | solution.py:153
  478.6 1.1 broadcast.243
  479.7 7.8 broadcast.245
  487.5 7.9 broadcast.244
  495.8 1.3 collective-permute-start.7
  497.1 15.8 %collective-permute-done.7 = bf16[128,4096]{1,0:T(8,128)(2,1)S(1)} collective-permute-done((bf16[128,4096]{1,0:T(8,128)(2,1)}, bf16[128,4096]{1,0:T(8,128)(2,1)S(1)}, u32[]{:S(2)}, u32[]{:S(2)}) %collective-permute-start.7) | collective-permute-done | bytes 1048608 | tf_op jit(solution)/shard_map/ppermute | solution.py:37
  513.0 16.1 %conditional.14 = (bf16[128,4096]{1,0:T(8,128)(2,1)S(1)}, f32[4096,1024]{1,0:T(8,128)}, f32[1024,4096]{1,0:T(8,128)}) conditional(s32[]{:T(128)} %convert_element_type.181, () %tuple.73, (pred[]{:T(512)}, bf16[128,4096]{1,0:T(8,128)(2,1)S(1)}, bf16[128,4096]{1,0:T(8,128)(2,1)S(1)}, bf16[128,4096]{1,0:T(8,128)(2,1)S(1)}, ...), branch_computations={%region_20.21_spmd, %region_21.24_spmd} | conditional | flops 5382078464 | bytes 136582752 | solution.py:153
  513.2 7.9 broadcast.251
  521.1 8.0 broadcast.250
  529.1 1.3 collective-permute-start.8
  530.4 41.1 %collective-permute-done.8 = bf16[128,4096]{1,0:T(8,128)(2,1)} collective-permute-done((bf16[128,4096]{1,0:T(8,128)(2,1)S(1)}, bf16[128,4096]{1,0:T(8,128)(2,1)}, u32[]{:S(2)}, u32[]{:S(2)}) %collective-permute-start.8) | collective-permute-done | bytes 1048608 | tf_op jit(solution)/shard_map/ppermute | solution.py:37
  571.4 31.9 %conditional.15 = (bf16[128,4096]{1,0:T(8,128)(2,1)}, f32[4096,1024]{1,0:T(8,128)}, f32[1024,4096]{1,0:T(8,128)}) conditional(s32[]{:T(128)} %convert_element_type.180, () %tuple.72, (pred[]{:T(512)}, bf16[128,4096]{1,0:T(8,128)(2,1)S(1)}, bf16[128,4096]{1,0:T(8,128)(2,1)}, bf16[128,4096]{1,0:T(8,128)(2,1)S(1)}, bf16[1024,4096]{1,0:T(8,128)(2,1)}, ...), branch_computations={%region_24.25_spmd, %region_25.28_spmd} | conditional | flops 5382078464 | bytes 136582752 | solution.py:153
  571.7 1.3 broadcast_select_fusion.3
  573.0 0.3 fusion.110
  573.3 4.8 fusion.115
  578.2 1.1 copy-done.13
  579.2 2.9 fusion.112
  582.2 3.0 fusion.105
  585.2 1.6 fusion.109
  586.8 8.1 fusion.117
  594.9 8.2 fusion.113
  603.3 25.8 %multiply_convert_fusion.12 = bf16[1024,4096]{1,0:T(8,128)(2,1)} fusion(f32[1024,4096]{1,0:T(8,128)} %get-tuple-element.155, f32[1024,4096]{1,0:T(8,128)} %get-tuple-element.154, f32[1024,4096]{1,0:T(8,128)} %get-tuple-element.152, f32[1024,4096]{1,0:T(8,128)} %get-tuple-element.153), kind=kLoop, calls=%fused_computation.144 | loop fusion | flops 20971520 | bytes 75497472 | tf_op jit(solution)/shard_map/convert_element_type | solution.py:166
  629.2 27.0 %multiply_convert_fusion.13 = bf16[4096,1024]{1,0:T(8,128)(2,1)} fusion(f32[4096,1024]{1,0:T(8,128)} %get-tuple-element.151, f32[4096,1024]{1,0:T(8,128)} %get-tuple-element.150, f32[4096,1024]{1,0:T(8,128)} %get-tuple-element.148, f32[4096,1024]{1,0:T(8,128)} %get-tuple-element.149), kind=kLoop, calls=%fused_computation.145 | loop fusion | flops 20971520 | bytes 75497472 | tf_op jit(solution)/shard_map/convert_element_type | solution.py:163
  656.3 1.1 conditional.11
  656.3 1.1 broadcast.234
  657.3 0.5 copy-done.5
  657.9 0.3 copy-done.7
  658.2 2.9 select_bitcast_fusion
  661.1 112.3 %reduce-scatter.5.cloned.1.call-done = bf16[1024,512]{1,0:T(8,128)(2,1)} async-done(((bf16[1024,4096]{1,0:T(8,128)(2,1)}), bf16[1024,512]{1,0:T(8,128)(2,1)}) %reduce-scatter.5.cloned.1.call-update) | async-done | bytes 1048592 | tf_op jit(solution)/shard_map/reduce_scatter | solution.py:165
  773.4 4.4 fusion.121
  777.8 145.8 %reduce-scatter.3.cloned.1.call-done = bf16[512,1024]{1,0:T(8,128)(2,1)} async-done(((bf16[4096,1024]{1,0:T(8,128)(2,1)}), bf16[512,1024]{1,0:T(8,128)(2,1)}) %reduce-scatter.3.cloned.1.call-update) | async-done | bytes 1048592 | tf_op jit(solution)/shard_map/reduce_scatter | solution.py:162
  923.7 3.7 fusion.125
  (42 shorter events, 1.0 us)
Async XLA Ops:
  7.2 3.1 copy-start
  7.2 380.2 %all-gather.2.cloned.1.call-start = ((), (), s32[]{:S(2)}) async-start(), calls=%async_computation.2 | async-start | bytes 9437184 | tf_op jit(solution)/shard_map/all_gather | solution.py:95
  10.2 763.2 %reduce-scatter.5.cloned.1.call-start = ((), (), s32[]{:S(2)}) async-start(), calls=%async_computation.4 | async-start | bytes 9437184 | tf_op jit(solution)/shard_map/reduce_scatter | solution.py:165
  10.5 37.5 %collective-permute-start = (bf16[1,512,1024]{2,1,0:T(8,128)(2,1)S(1)}, bf16[1,512,1024]{2,1,0:T(8,128)(2,1)}, u32[]{:S(2)}, u32[]{:S(2)}) collective-permute-start(bf16[1,512,1024]{2,1,0:T(8,128)(2,1)S(1)} %multiply_convert_fusion.14), channel_id=1, source_target_pairs={{0,1},{1,0},{2,3},{3,2},{4,5},{5,4},{6,7},{7,6},{8,9},{9,8},{10,11... | collective-permute-start | bytes 3145736 | tf_op jit(solution)/shard_map/ppermute | solution.py:23
  51.7 97.4 %collective-permute-start.1 = (bf16[2,512,1024]{2,1,0:T(8,128)(2,1)}, bf16[2,512,1024]{2,1,0:T(8,128)(2,1)}, u32[]{:S(2)}, u32[]{:S(2)}) collective-permute-start(bf16[2,512,1024]{2,1,0:T(8,128)(2,1)} %get-tuple-element.167), channel_id=1, source_target_pairs={{0,2},{1,3},{2,0},{3,1},{4,6},{5,7},{6,4},{7,5},{8,10},{9,11},{10,... | collective-permute-start | bytes 6291464 | tf_op jit(solution)/shard_map/ppermute | solution.py:23
  151.0 3.4 copy-start.3
  154.2 211.9 %collective-permute-start.2 = (bf16[4,512,1024]{2,1,0:T(8,128)(2,1)}, bf16[4,512,1024]{2,1,0:T(8,128)(2,1)}, u32[]{:S(2)}, u32[]{:S(2)}) collective-permute-start(bf16[4,512,1024]{2,1,0:T(8,128)(2,1)} %bitcast.6), channel_id=1, source_target_pairs={{0,4},{1,5},{2,6},{3,7},{4,0},{5,1},{6,2},{7,3},{8,12},{9,13},{10,... | collective-permute-start | bytes 12582920 | tf_op jit(solution)/shard_map/ppermute | solution.py:23
  395.9 4.8 copy-start.6
  395.9 3.7 collective-permute-start.3
  400.9 18.7 %copy-start.8 = (bf16[128,4096]{1,0:T(8,128)(2,1)}, bf16[128,4096]{1,0:T(8,128)(2,1)S(1)}, u32[]{:S(2)}) copy-start(bf16[128,4096]{1,0:T(8,128)(2,1)S(1)} %get-tuple-element.195) | copy-start | bytes 3145732
  400.9 17.6 %collective-permute-start.4 = (bf16[128,4096]{1,0:T(8,128)(2,1)S(1)}, bf16[128,4096]{1,0:T(8,128)(2,1)S(1)}, u32[]{:S(2)}, u32[]{:S(2)}) collective-permute-start(bf16[128,4096]{1,0:T(8,128)(2,1)S(1)} %get-tuple-element.195), channel_id=1, source_target_pairs={{0,8},{8,16},{16,24},{1,9},{9,17},{17,25},{2,10},{10,18},{18,26},{... | collective-permute-start | bytes 3145736 | tf_op jit(solution)/shard_map/ppermute | solution.py:37
  419.7 12.4 %copy-start.9 = (bf16[128,4096]{1,0:T(8,128)(2,1)}, bf16[128,4096]{1,0:T(8,128)(2,1)S(1)}, u32[]{:S(2)}) copy-start(bf16[128,4096]{1,0:T(8,128)(2,1)S(1)} %get-tuple-element.196) | copy-start | bytes 3145732
  419.7 13.8 %collective-permute-start.5 = (bf16[128,4096]{1,0:T(8,128)(2,1)S(1)}, bf16[128,4096]{1,0:T(8,128)(2,1)}, u32[]{:S(2)}, u32[]{:S(2)}) collective-permute-start(bf16[128,4096]{1,0:T(8,128)(2,1)S(1)} %get-tuple-element.196), channel_id=1, source_target_pairs={{0,8},{8,16},{16,24},{1,9},{9,17},{17,25},{2,10},{10,18},{18,26},{... | collective-permute-start | bytes 3145736 | tf_op jit(solution)/shard_map/ppermute | solution.py:37
  432.1 2.7 copy-start.2
  450.8 27.8 %copy-start.4 = (bf16[128,4096]{1,0:T(8,128)(2,1)}, bf16[128,4096]{1,0:T(8,128)(2,1)S(1)}, u32[]{:S(2)}) copy-start(bf16[128,4096]{1,0:T(8,128)(2,1)S(1)} %get-tuple-element.144) | copy-start | bytes 3145732
  450.8 27.8 %collective-permute-start.6 = (bf16[128,4096]{1,0:T(8,128)(2,1)S(1)}, bf16[128,4096]{1,0:T(8,128)(2,1)}, u32[]{:S(2)}, u32[]{:S(2)}) collective-permute-start(bf16[128,4096]{1,0:T(8,128)(2,1)S(1)} %get-tuple-element.144), channel_id=1, source_target_pairs={{8,0},{16,8},{24,16},{9,1},{17,9},{25,17},{10,2},{18,10},{26,18},{... | collective-permute-start | bytes 3145736 | tf_op jit(solution)/shard_map/ppermute | solution.py:37
  495.8 17.2 %collective-permute-start.7 = (bf16[128,4096]{1,0:T(8,128)(2,1)}, bf16[128,4096]{1,0:T(8,128)(2,1)S(1)}, u32[]{:S(2)}, u32[]{:S(2)}) collective-permute-start(bf16[128,4096]{1,0:T(8,128)(2,1)} %get-tuple-element.145), channel_id=1, source_target_pairs={{8,0},{16,8},{24,16},{9,1},{17,9},{25,17},{10,2},{18,10},{26,18},{... | collective-permute-start | bytes 3145736 | tf_op jit(solution)/shard_map/ppermute | solution.py:37
  529.1 42.4 %collective-permute-start.8 = (bf16[128,4096]{1,0:T(8,128)(2,1)S(1)}, bf16[128,4096]{1,0:T(8,128)(2,1)}, u32[]{:S(2)}, u32[]{:S(2)}) collective-permute-start(bf16[128,4096]{1,0:T(8,128)(2,1)S(1)} %get-tuple-element.146), channel_id=1, source_target_pairs={{8,0},{16,8},{24,16},{9,1},{17,9},{25,17},{10,2},{18,10},{26,18},{... | collective-permute-start | bytes 3145736 | tf_op jit(solution)/shard_map/ppermute | solution.py:37
  573.0 9.2 slice-start.6
  573.3 5.9 copy-start.13
  573.3 8.9 slice-start.7
  629.1 294.6 %reduce-scatter.3.cloned.1.call-start = ((), (), s32[]{:S(2)}) async-start(), calls=%async_computation.3 | async-start | bytes 9437184 | tf_op jit(solution)/shard_map/reduce_scatter | solution.py:162
  656.2 1.6 copy-start.5
  656.2 2.0 copy-start.7
  661.1 262.6 %copy-start.1 = (f32[1,512,1024]{2,1,0:T(8,128)S(1)}, f32[1,512,1024]{2,1,0:T(8,128)}, u32[]{:S(2)}) copy-start(f32[1,512,1024]{2,1,0:T(8,128)} %param.24) | copy-start | bytes 6291460
Sparse Core Ops, SparseCore 0:
  10.6 283.7 all-gather.1
  629.2 144.1 reduce-scatter.4
  777.1 146.5 reduce-scatter.2
